TPU v7x, 32 devices: a whole 2x2x4 slice. The times are simulated.
32 devices in a mesh: tensor: 4 (over z), example: 8 (over y, x, core).
Axes of the slice: x: 2, y: 2, z: 4, core: 2. Of those that a mesh axis runs over, the one named last changes fastest.
Arguments:
- queries: bfloat16 [1, 4096, 4096], P(None, 'example', 'tensor'), may hold values from -0.0014648438 to 0.0014648438
- basis_out: bfloat16 [4096, 4096], P('example', 'tensor'), may hold values from -0.09375 to 0.09375
- basis_in: bfloat16 [4096, 4096], P('tensor', 'example'), may hold values from -0.09375 to 0.09375
- eigvals: float32 [4096, 4096], P('tensor', 'example'), may hold values from 0.25 to 4
- input_fac: bfloat16 [128, 8, 4096], P('example', None, 'tensor'), may hold values from -6 to 6
- grad_fac: bfloat16 [128, 8, 4096], P('example', None, 'tensor'), may hold values from -6 to 6
- cand_slot: int32 [128], replicated, may hold values from 0 to 127, as said below
- score_list: int32 [8, 16], replicated, may hold values from 0 to 127, as said below
- token_count: int32 [128], replicated, may hold values from 1 to 8
Outputs:
- scores: float32 [1, 128, 8], P(None, 'example')
Inputs may be any that keep to these rules, and one draw needn't show every extreme that they name: `cand_slot`: a permutation; slot s belongs to owner s // 16. `score_list`: every candidate appears exactly once; a scorer's list holds at most 4 candidates of any one owner, and some scorer takes exactly 4 from some owner.
All inputs are finite; a program needn't handle non-finite values.
Results may differ from a plain program's by a relative error of at most 0.019.
Values may be sent and summed in bfloat16 or wider, within the bound.
A program may use at most 128 MiB of HBM per device.

v0:
```python
import jax
import jax.numpy as jnp
from jax import lax
from jax.sharding import PartitionSpec as P


def body(
    queries, basis_out, basis_in, eigvals, input_fac, grad_fac, cand_slot, score_list, token_count
):
    ex_count = lax.axis_size("example")
    my_index = lax.axis_index("example")
    out_rows = lax.all_gather(basis_out, "tensor", axis=1, tiled=True)
    in_rows = lax.all_gather(basis_in, "example", axis=1, tiled=True)
    query_total = queries.shape[0]
    columns = out_rows
    rotated = lax.psum_scatter(
        jnp.einsum("ki,qkj->iqj", columns, queries, preferred_element_type=jnp.float32).astype(
            jnp.bfloat16
        ),
        "example",
        scatter_dimension=0,
        tiled=True,
    )
    columns = in_rows
    core_sum = lax.psum_scatter(
        jnp.einsum("kj,iqk->jqi", columns, rotated, preferred_element_type=jnp.float32).astype(
            jnp.bfloat16
        ),
        "tensor",
        scatter_dimension=0,
        tiled=True,
    ).astype(jnp.float32)
    scaled = (core_sum / eigvals[:, None, :]).astype(jnp.bfloat16)
    columns = out_rows
    turned = jnp.einsum(
        "jqk,ik->jqi",
        lax.all_gather(scaled, "example", axis=2, tiled=True),
        columns,
        preferred_element_type=jnp.float32,
    ).astype(jnp.bfloat16)
    columns = in_rows
    precond = jnp.einsum(
        "jk,kqi->jqi",
        columns,
        lax.all_gather(turned, "tensor", axis=0, tiled=True),
        preferred_element_type=jnp.float32,
    ).astype(jnp.bfloat16)
    cand_total = cand_slot.shape[0]
    cand_dev = input_fac.shape[0]
    token_len = input_fac.shape[1]
    shard_width = input_fac.shape[2]
    list_len = score_list.shape[1]
    cand_ids = jnp.arange(cand_total, dtype=jnp.int32)
    matches = (score_list[:, :, None] == cand_ids[None, None, :]).astype(jnp.int32)
    entry_slot = jnp.sum(matches * cand_slot[None, None, :], axis=2)
    entry_count = jnp.sum(matches * token_count[None, None, :], axis=2)
    entry_owner = entry_slot // cand_dev
    entry_local = entry_slot % cand_dev
    earlier = jnp.arange(list_len)[:, None] > jnp.arange(list_len)[None, :]
    same_owner = entry_owner[:, :, None] == entry_owner[:, None, :]
    entry_rank = jnp.sum((same_owner & earlier[None]).astype(jnp.int32), axis=2)
    capacity = 2 * cand_dev // ex_count
    place_ids = jnp.arange(capacity, dtype=jnp.int32)
    local_ids = jnp.arange(cand_dev, dtype=jnp.int32)
    owned_here = entry_owner == my_index
    send_table = jnp.sum(
        (
            owned_here[:, :, None, None]
            & (entry_rank[:, :, None, None] == place_ids[None, None, :, None])
            & (entry_local[:, :, None, None] == local_ids[None, None, None, :])
        ).astype(jnp.float32),
        axis=1,
    )
    my_owner = lax.dynamic_index_in_dim(entry_owner, my_index, 0, keepdims=False)
    my_rank = lax.dynamic_index_in_dim(entry_rank, my_index, 0, keepdims=False)
    my_count = lax.dynamic_index_in_dim(entry_count, my_index, 0, keepdims=False)
    source_ids = jnp.arange(ex_count, dtype=jnp.int32)
    take_table = (
        (
            (my_owner[:, None, None] == source_ids[None, :, None])
            & (my_rank[:, None, None] == place_ids[None, None, :])
        )
        .astype(jnp.float32)
        .reshape(list_len, ex_count * capacity)
    )
    select_send = send_table.astype(jnp.bfloat16)
    select_take = take_table.astype(jnp.bfloat16)

    def route_rows(owned_rows):
        return jnp.einsum(
            "ers,sx->erx", select_send, owned_rows, preferred_element_type=jnp.float32
        ).astype(jnp.bfloat16)

    def collect_rows(received):
        flat_received = received.reshape(ex_count * capacity, received.shape[2])
        return jnp.dot(select_take, flat_received, preferred_element_type=jnp.float32).astype(
            jnp.bfloat16
        )

    flat_acts = input_fac.reshape(cand_dev, token_len * shard_width)
    flat_grads = grad_fac.reshape(cand_dev, token_len * shard_width)
    sent_acts, sent_grads = (
        lax.all_to_all(route_rows(flat_acts), "example", split_axis=0, concat_axis=0, tiled=True),
        lax.all_to_all(route_rows(flat_grads), "example", split_axis=0, concat_axis=0, tiled=True),
    )
    got_acts = collect_rows(sent_acts).reshape(list_len * token_len, shard_width)
    got_grads = collect_rows(sent_grads).reshape(list_len * token_len, shard_width)
    whole_grads = lax.all_gather(got_grads, "tensor", axis=1, tiled=True)
    columns = whole_grads
    weighted = jnp.einsum(
        "tn,jqn->qtj",
        columns,
        lax.all_gather(precond, "example", axis=2, tiled=True),
        preferred_element_type=jnp.float32,
    )
    partial_scores = jnp.sum(got_acts.astype(jnp.float32)[None] * weighted, axis=2)
    summed = lax.psum(partial_scores, "tensor").reshape(query_total, list_len, token_len)
    live_mask = jnp.arange(token_len, dtype=jnp.int32)[None, :] < my_count[:, None]
    return jnp.where(live_mask[None], summed, jnp.float32(0.0))


def solution(mesh):
    in_specs = (
        P(None, "example", "tensor"),
        P("example", "tensor"),
        P("tensor", "example"),
        P("tensor", "example"),
        P("example", None, "tensor"),
        P("example", None, "tensor"),
        P(),
        P(),
        P(),
    )
    out_specs = P(None, "example", None)
    return jax.shard_map(body, mesh=mesh, in_specs=in_specs, out_specs=out_specs, check_vma=False)
```

profile of v0, /device:TPU:0, one launch (start us, length us, event | category | flops | bytes accessed | tf_op | source)
XLA Modules:
  0.0 568.8 jit_solution(2000959011714621672)
XLA Ops:
  6.5 0.7 all-gather.9.cloned.1.call-update
  7.3 0.0 all-gather.11.cloned.1.call-start
  7.3 0.7 all-gather.11.cloned.1.call-update
  8.0 0.0 reduce-scatter.3.cloned.1.call-start
  8.1 84.4 %all-gather.9.cloned.1.call-done = bf16[512,4096]{1,0:T(8,128)(2,1)} async-done(((bf16[512,1024]{1,0:T(8,128)(2,1)}), bf16[512,4096]{1,0:T(8,128)(2,1)}) %all-gather.9.cloned.1.call-update) | async-done | bytes 4194320 | tf_op jit(solution)/shard_map/all_gather | solution.py:12
  92.4 9.0 %convert_bitcast_fusion = bf16[4096,1,1024]{2,0,1:T(8,128)(2,1)} fusion(bf16[512,4096]{1,0:T(8,128)(2,1)} %all-gather.9.cloned.1.call-done, bf16[1,512,1024]{2,1,0:T(8,128)(2,1)S(1)} %copy-done), kind=kOutput, calls=%fused_computation.9 | convolution fusion | flops 4299161600 | bytes 13631488 | tf_op jit(solution)/shard_map/ki,qkj->iqj/dot_general | solution.py:17
  101.4 0.0 reduce-scatter.5.cloned.1.call-start
  101.5 47.3 %all-gather.11.cloned.1.call-done = bf16[1024,4096]{1,0:T(8,128)(2,1)} async-done(((bf16[1024,512]{1,0:T(8,128)(2,1)}), bf16[1024,4096]{1,0:T(8,128)(2,1)}) %all-gather.11.cloned.1.call-update) | async-done | bytes 8388624 | tf_op jit(solution)/shard_map/all_gather | solution.py:13
  148.8 74.8 %reduce-scatter.3.cloned.1.call-done = bf16[512,1,1024]{2,0,1:T(8,128)(2,1)} async-done(((bf16[4096,1,1024]{2,0,1:T(8,128)(2,1)}), bf16[512,1,1024]{2,0,1:T(8,128)(2,1)}) %reduce-scatter.3.cloned.1.call-update) | async-done | bytes 1048592 | tf_op jit(solution)/shard_map/reduce_scatter | solution.py:16
  223.6 10.2 %fusion.5 = bf16[4096,1,512]{0,2,1:T(8,128)(2,1)} fusion(bf16[1024,4096]{1,0:T(8,128)(2,1)} %all-gather.11.cloned.1.call-done, bf16[512,1,1024]{2,0,1:T(8,128)(2,1)} %reduce-scatter.3.cloned.1.call-done), kind=kOutput, calls=%fused_computation.11 | convolution fusion | flops 4297064448 | bytes 13631488 | tf_op jit(solution)/shard_map/kj,iqk->jqi/dot_general | solution.py:26
  233.8 0.0 reduce-scatter.5.cloned.1.call-update
  233.8 0.0 all-gather.13.cloned.1.call-start
  233.9 1.9 copy.26
  235.8 74.9 %reduce-scatter.5.cloned.1.call-done = bf16[1024,1,512]{0,2,1:T(8,128)(2,1)} async-done(((bf16[4096,1,512]{0,2,1:T(8,128)(2,1)}), bf16[1024,1,512]{0,2,1:T(8,128)(2,1)}) %reduce-scatter.5.cloned.1.call-update) | async-done | bytes 1048592 | tf_op jit(solution)/shard_map/reduce_scatter | solution.py:25
  310.7 2.6 fusion.6
  313.4 0.2 all-gather.17.cloned.1.call-start
  313.6 54.8 %all-gather.13.cloned.1.call-done = bf16[1024,1,4096]{0,2,1:T(8,128)(2,1)} async-done(((bf16[1024,1,512]{0,2,1:T(8,128)(2,1)}), bf16[1024,1,4096]{0,2,1:T(8,128)(2,1)}) %all-gather.13.cloned.1.call-update) | async-done | bytes 8388624 | tf_op jit(solution)/shard_map/all_gather | solution.py:37
  368.4 10.1 %fusion.7 = bf16[1024,512]{1,0:T(8,128)(2,1)} fusion(bf16[512,4096]{1,0:T(8,128)(2,1)} %all-gather.9.cloned.1.call-done, bf16[1024,1,4096]{0,2,1:T(8,128)(2,1)} %all-gather.13.cloned.1.call-done), kind=kOutput, calls=%fused_computation.14 | convolution fusion | flops 4295491584 | bytes 13631488 | tf_op jit(solution)/shard_map/jqk,ik->jqi/dot_general | solution.py:35
  378.5 0.1 reshape.275
  378.7 0.4 select_reduce_fusion.1
  379.1 0.3 convert_reduce_fusion.1
  379.5 0.1 iota_compare_fusion
  379.5 0.2 convert_reduce_fusion
  379.7 0.3 convolution_convert_fusion
  380.0 1.2 copy.28
  381.2 3.5 all-to-all-start.1
  384.7 0.0 all-gather.15.cloned.1.call-start
  384.8 9.6 %all-to-all-done.1 = bf16[8,4,8192]{2,1,0:T(4,128)(2,1)S(1)} async-done(((bf16[8,4,8192]{2,1,0:T(4,128)(2,1)}), bf16[8,4,8192]{2,1,0:T(4,128)(2,1)S(1)}, u32[]{:S(2)}, u32[]{:S(2)}) %all-to-all-start.1) | async-done | bytes 524320 | tf_op jit(solution)/shard_map/all_to_all | solution.py:104
  394.4 0.4 fusion.2
  394.8 0.9 reshape.265
  395.7 0.3 all-gather.19.cloned.1.call-start
  396.0 63.5 %all-gather.17.cloned.1.call-done = bf16[4096,512]{1,0:T(8,128)(2,1)} async-done(((bf16[1024,512]{1,0:T(8,128)(2,1)}), bf16[4096,512]{1,0:T(8,128)(2,1)}) %all-gather.17.cloned.1.call-update) | async-done | bytes 4194320 | tf_op jit(solution)/shard_map/all_gather | solution.py:45
  459.4 10.2 %fusion.10 = bf16[1024,512]{0,1:T(8,128)(2,1)} fusion(bf16[4096,512]{1,0:T(8,128)(2,1)} %all-gather.17.cloned.1.call-done, bf16[1024,4096]{1,0:T(8,128)(2,1)} %all-gather.11.cloned.1.call-done), kind=kOutput, calls=%fused_computation.16 | convolution fusion | flops 4295491584 | bytes 13631488 | tf_op jit(solution)/shard_map/jk,kqi->jqi/dot_general | solution.py:42
  469.6 0.1 reshape.273
  469.8 0.3 convolution_convert_fusion.1
  470.1 1.2 copy.24
  471.3 3.7 all-to-all-start
  475.0 9.7 %all-to-all-done = bf16[8,4,8192]{2,1,0:T(4,128)(2,1)S(1)} async-done(((bf16[8,4,8192]{2,1,0:T(4,128)(2,1)}), bf16[8,4,8192]{2,1,0:T(4,128)(2,1)S(1)}, u32[]{:S(2)}, u32[]{:S(2)}) %all-to-all-start) | async-done | bytes 524320 | tf_op jit(solution)/shard_map/all_to_all | solution.py:103
  484.7 0.4 fusion.1
  485.1 0.1 reshape.268
  485.3 0.2 copy.30
  485.4 2.0 all-gather.15.cloned.1.call-done
  487.5 55.8 %all-gather.19.cloned.1.call-done = bf16[1024,4096]{0,1:T(8,128)(2,1)} async-done(((bf16[1024,512]{0,1:T(8,128)(2,1)}), bf16[1024,4096]{0,1:T(8,128)(2,1)}) %all-gather.19.cloned.1.call-update) | async-done | bytes 8388624 | tf_op jit(solution)/shard_map/all_gather | solution.py:113
  543.3 6.0 %fusion.12 = f32[128]{0:T(128)S(1)} fusion(f32[1,128,1024]{1,2,0:T(8,128)S(1)} %copy.30, bf16[1024,4096]{0,1:T(8,128)(2,1)} %all-gather.19.cloned.1.call-done, bf16[128,4096]{1,0:T(8,128)(2,1)} %all-gather.15.cloned.1.call-done), kind=kOutput, calls=%fused_computation.19 | convolution fusion | flops 1074003840 | bytes 9961984 | tf_op jit(solution)/shard_map/tn,jqn->qtj/dot_general | solution.py:110
  549.3 0.1 reshape.266
  549.4 11.8 %psum.7 = f32[1,16,8]{2,1,0:T(8,128)S(1)} all-reduce(f32[1,16,8]{2,1,0:T(8,128)S(1)} %reshape.266), channel_id=1, replica_groups=mesh['tensor'=4,'example'=8] {'tensor'}, use_global_device_ids=true, to_apply=%region_7.8 | all-reduce | flops 128 | bytes 1024 | tf_op jit(solution)/shard_map/psum | solution.py:117
  561.2 0.1 fusion.18
  561.3 0.7 copy.31
  (26 shorter events, 0.2 us)
Async XLA Ops:
  6.5 85.9 %copy-start = (bf16[1,512,1024]{2,1,0:T(8,128)(2,1)S(1)}, bf16[1,512,1024]{2,1,0:T(8,128)(2,1)}, u32[]{:S(2)}) copy-start(bf16[1,512,1024]{2,1,0:T(8,128)(2,1)} %param.9) | copy-start | bytes 3145732
  6.5 85.9 %all-gather.9.cloned.1.call-start = ((), (), s32[]{:S(2)}) async-start(), calls=%async_computation.4 | async-start | bytes 5242880 | tf_op jit(solution)/shard_map/all_gather | solution.py:12
  7.3 141.6 %all-gather.11.cloned.1.call-start = ((), (), s32[]{:S(2)}) async-start(), calls=%async_computation.6 | async-start | bytes 9437184 | tf_op jit(solution)/shard_map/all_gather | solution.py:13
  8.0 215.6 %reduce-scatter.3.cloned.1.call-start = ((), (), s32[]{:S(2)}) async-start(), calls=%async_computation.5 | async-start | bytes 9437184 | tf_op jit(solution)/shard_map/reduce_scatter | solution.py:16
  101.4 209.3 %reduce-scatter.5.cloned.1.call-start = ((), (), s32[]{:S(2)}) async-start(), calls=%async_computation.7 | async-start | bytes 5242880 | tf_op jit(solution)/shard_map/reduce_scatter | solution.py:25
  233.8 134.6 %all-gather.13.cloned.1.call-start = ((), (), s32[]{:S(2)}) async-start(), calls=%async_computation.8 | async-start | bytes 9437184 | tf_op jit(solution)/shard_map/all_gather | solution.py:37
  313.4 65.1 %copy-start.1 = (bf16[16,8,1024]{2,1,0:T(8,128)(2,1)S(1)}, bf16[16,8,1024]{2,1,0:T(8,128)(2,1)}, u32[]{:S(2)}) copy-start(bf16[16,8,1024]{2,1,0:T(8,128)(2,1)} %param.14) | copy-start | bytes 786436
  313.4 65.3 %copy-start.3 = (s32[8,16]{1,0:T(8,128)S(1)}, s32[8,16]{1,0:T(8,128)}, u32[]{:S(2)}) copy-start(s32[8,16]{1,0:T(8,128)} %param.16) | copy-start | bytes 1540
  313.4 65.3 %copy-start.4 = (s32[128]{0:T(128)S(1)}, s32[128]{0:T(128)}, u32[]{:S(2)}) copy-start(s32[128]{0:T(128)} %param.17) | copy-start | bytes 1540
  313.4 65.3 %copy-start.5 = (s32[128]{0:T(128)S(1)}, s32[128]{0:T(128)}, u32[]{:S(2)}) copy-start(s32[128]{0:T(128)} %param.15) | copy-start | bytes 1540
  313.4 146.0 %all-gather.17.cloned.1.call-start = ((), (), s32[]{:S(2)}) async-start(), calls=%async_computation.10 | async-start | bytes 5242880 | tf_op jit(solution)/shard_map/all_gather | solution.py:45
  381.2 13.2 %all-to-all-start.1 = ((bf16[8,4,8192]{2,1,0:T(4,128)(2,1)}), bf16[8,4,8192]{2,1,0:T(4,128)(2,1)S(1)}, u32[]{:S(2)}, u32[]{:S(2)}) async-start(bf16[8,4,8192]{2,1,0:T(4,128)(2,1)} %copy.28), calls=%async_computation.3 | async-start | bytes 1048576 | tf_op jit(solution)/shard_map/all_to_all | solution.py:104
  384.7 102.8 %all-gather.15.cloned.1.call-start = ((), (), s32[]{:S(2)}) async-start(), calls=%async_computation.9 | async-start | bytes 1310720 | tf_op jit(solution)/shard_map/all_gather | solution.py:108
  395.7 74.0 %copy-start.2 = (bf16[16,8,1024]{2,1,0:T(8,128)(2,1)S(1)}, bf16[16,8,1024]{2,1,0:T(8,128)(2,1)}, u32[]{:S(2)}) copy-start(bf16[16,8,1024]{2,1,0:T(8,128)(2,1)} %param.13) | copy-start | bytes 786436
  395.7 147.6 %all-gather.19.cloned.1.call-start = ((), (), s32[]{:S(2)}) async-start(), calls=%async_computation.11 | async-start | bytes 9437184 | tf_op jit(solution)/shard_map/all_gather | solution.py:113
  471.3 13.4 %all-to-all-start = ((bf16[8,4,8192]{2,1,0:T(4,128)(2,1)}), bf16[8,4,8192]{2,1,0:T(4,128)(2,1)S(1)}, u32[]{:S(2)}, u32[]{:S(2)}) async-start(bf16[8,4,8192]{2,1,0:T(4,128)(2,1)} %copy.24), calls=%async_computation | async-start | bytes 1048576 | tf_op jit(solution)/shard_map/all_to_all | solution.py:103
Sparse Core Ops, SparseCore 0:
  8.9 83.4 all-gather.8
  94.3 54.4 all-gather.10
  152.3 71.2 reduce-scatter.2
  233.9 76.7 reduce-scatter.4
  313.5 54.8 all-gather.12
  378.6 80.7 all-gather.16
  461.0 26.4 all-gather.14
  489.4 53.8 all-gather.18
where the time goes:
time: 569 us
  waiting for transfers between devices  478 us (84%)
  matrix products  46.8 us (8%)
  between operations  13.7 us (2%)
  blocking collectives  11.8 us (2%)
  starting transfers between devices  7.87 us (1%)
  local copies, waits for them, and re-layouts  6.58 us (1%)
    all_gather x1, waiting for transfers between devices, body(): out_rows = lax.all_gather(basis_out, 'tensor', axis=1, tiled=True)  84.4 us
    reduce_scatter x1, waiting for transfers between devices, body(): lax.psum_scatter(jnp.einsum('kj,iqk->jqi', columns, rotated, preferred_el...  74.9 us
    reduce_scatter x1, waiting for transfers between devices, body(): lax.psum_scatter(jnp.einsum('ki,qkj->iqj', columns, queries, preferred_el...  74.8 us
    all_gather x1, waiting for transfers between devices, body(): lax.all_gather(turned, 'tensor', axis=0, tiled=True)  63.5 us
    all_gather x1, waiting for transfers between devices, body(): lax.all_gather(precond, 'example', axis=2, tiled=True)  55.8 us
    all_gather x1, waiting for transfers between devices, body(): lax.all_gather(scaled, 'example', axis=2, tiled=True)  54.8 us
    all_gather x1, waiting for transfers between devices, body(): in_rows = lax.all_gather(basis_in, 'example', axis=1, tiled=True)  47.3 us
    psum x1, blocking collectives, body(): lax.psum(partial_scores, 'tensor').reshape(query_total, list_len, token_len)  11.8 us
  transfers between devices with their start and end apart: 10, of which 10 were waited for; matrix products, arithmetic and copies ran while one was open for 5% of the time, Pallas kernels for 0%

commit v1 on v0

--- a/solution.py
+++ b/solution.py
@@ -2,6 +2,19 @@
 import jax.numpy as jnp
 from jax import lax
 from jax.sharding import PartitionSpec as P
+
+
+def ring_gather(x, axis, dim):
+    ways = lax.axis_size(axis)
+    up = [(d, (d + 1) % ways) for d in range(ways)]
+    down = [(d, (d - 1) % ways) for d in range(ways)]
+    earlier, later = ([x], [x])
+    for _ in range(ways // 2):
+        earlier.append(lax.ppermute(earlier[-1], axis, up))
+    for _ in range((ways - 1) // 2):
+        later.append(lax.ppermute(later[-1], axis, down))
+    line = jnp.concatenate([*earlier[::-1], *later[1:]], axis=dim)
+    return jnp.roll(line, (lax.axis_index(axis) - ways // 2) * x.shape[dim], axis=dim)
 
 
 def body(
@@ -34,7 +47,7 @@
     columns = out_rows
     turned = jnp.einsum(
         "jqk,ik->jqi",
-        lax.all_gather(scaled, "example", axis=2, tiled=True),
+        ring_gather(scaled, "example", 2),
         columns,
         preferred_element_type=jnp.float32,
     ).astype(jnp.bfloat16)

time: 569 us -> 615 us (1.081)
  waiting for transfers between devices: 478 us -> 507 us
  local copies, waits for them, and re-layouts: 6.58 us -> 18.8 us
  starting transfers between devices: 7.87 us -> 15.7 us
    ppermute x0 -> x7, waiting for transfers between devices: none -> 85.2 us  [the longest x4 85.2 us: ring_gather(): earlier.append(lax.ppermute(earlier[-1], axis, up))]
    all_gather x1 -> x0, waiting for transfers between devices: 54.8 us -> none  [body(): lax.all_gather(scaled, 'example', axis=2, tiled=True)]
    unnamed x13 -> x34, local copies, waits for them, and re-layouts: 1.96 us -> 12.8 us
    ppermute x0 -> x7, starting transfers between devices: none -> 7.99 us  [the longest x3 7.92 us: ring_gather(): later.append(lax.ppermute(later[-1], axis, down))]
  transfers between devices with their start and end apart: 10 -> 16, of which waited for: 10 -> 13; matrix products, arithmetic and copies ran while one was open for 5% -> 5% of each run, Pallas kernels for 0% -> 0%
where the time goes in v1:
time: 615 us
  waiting for transfers between devices  507 us (82%)
  matrix products  44.6 us (7%)
  local copies, waits for them, and re-layouts  18.8 us (3%)
  starting transfers between devices  15.7 us (3%)
  between operations  13.8 us (2%)
  blocking collectives  11.8 us (2%)
    ppermute x4, waiting for transfers between devices, ring_gather(): earlier.append(lax.ppermute(earlier[-1], axis, up))  85.2 us
    all_gather x1, waiting for transfers between devices, body(): out_rows = lax.all_gather(basis_out, 'tensor', axis=1, tiled=True)  84.4 us
    reduce_scatter x1, waiting for transfers between devices, body(): lax.psum_scatter(jnp.einsum('kj,iqk->jqi', columns, rotated, preferred_el...  74.9 us
    reduce_scatter x1, waiting for transfers between devices, body(): lax.psum_scatter(jnp.einsum('ki,qkj->iqj', columns, queries, preferred_el...  74.8 us
    all_gather x1, waiting for transfers between devices, body(): lax.all_gather(turned, 'tensor', axis=0, tiled=True)  62.1 us
    all_gather x1, waiting for transfers between devices, body(): lax.all_gather(precond, 'example', axis=2, tiled=True)  55.8 us
    all_gather x1, waiting for transfers between devices, body(): in_rows = lax.all_gather(basis_in, 'example', axis=1, tiled=True)  47.3 us
    unnamed x34, local copies, waits for them, and re-layouts  12.8 us
  transfers between devices with their start and end apart: 16, of which 13 were waited for; matrix products, arithmetic and copies ran while one was open for 5% of the time, Pallas kernels for 0%

profile of v1, /device:TPU:0, one launch (start us, length us, event | category | flops | bytes accessed | tf_op | source)
XLA Modules:
  0.0 614.6 jit_solution(9621458897676860353)
XLA Ops:
  6.5 0.7 all-gather.8.cloned.1.call-update
  7.3 0.7 all-gather.10.cloned.1.call-update
  8.1 84.4 %all-gather.8.cloned.1.call-done = bf16[512,4096]{1,0:T(8,128)(2,1)} async-done(((bf16[512,1024]{1,0:T(8,128)(2,1)}), bf16[512,4096]{1,0:T(8,128)(2,1)}) %all-gather.8.cloned.1.call-update) | async-done | bytes 4194320 | tf_op jit(solution)/shard_map/all_gather | solution.py:25
  92.4 9.0 %convert_bitcast_fusion = bf16[4096,1,1024]{2,0,1:T(8,128)(2,1)} fusion(bf16[512,4096]{1,0:T(8,128)(2,1)} %all-gather.8.cloned.1.call-done, bf16[1,512,1024]{2,1,0:T(8,128)(2,1)S(1)} %copy-done), kind=kOutput, calls=%fused_computation.10 | convolution fusion | flops 4299161600 | bytes 13631488 | tf_op jit(solution)/shard_map/ki,qkj->iqj/dot_general | solution.py:30
  101.5 47.3 %all-gather.10.cloned.1.call-done = bf16[1024,4096]{1,0:T(8,128)(2,1)} async-done(((bf16[1024,512]{1,0:T(8,128)(2,1)}), bf16[1024,4096]{1,0:T(8,128)(2,1)}) %all-gather.10.cloned.1.call-update) | async-done | bytes 8388624 | tf_op jit(solution)/shard_map/all_gather | solution.py:26
  148.8 74.8 %reduce-scatter.3.cloned.1.call-done = bf16[512,1,1024]{2,0,1:T(8,128)(2,1)} async-done(((bf16[4096,1,1024]{2,0,1:T(8,128)(2,1)}), bf16[512,1,1024]{2,0,1:T(8,128)(2,1)}) %reduce-scatter.3.cloned.1.call-update) | async-done | bytes 1048592 | tf_op jit(solution)/shard_map/reduce_scatter | solution.py:29
  223.6 10.2 %fusion.6 = bf16[4096,1,512]{0,2,1:T(8,128)(2,1)} fusion(bf16[1024,4096]{1,0:T(8,128)(2,1)} %all-gather.10.cloned.1.call-done, bf16[512,1,1024]{2,0,1:T(8,128)(2,1)} %reduce-scatter.3.cloned.1.call-done), kind=kOutput, calls=%fused_computation.12 | convolution fusion | flops 4297064448 | bytes 13631488 | tf_op jit(solution)/shard_map/kj,iqk->jqi/dot_general | solution.py:39
  233.9 1.9 copy.26
  235.8 74.9 %reduce-scatter.5.cloned.1.call-done = bf16[1024,1,512]{0,2,1:T(8,128)(2,1)} async-done(((bf16[4096,1,512]{0,2,1:T(8,128)(2,1)}), bf16[1024,1,512]{0,2,1:T(8,128)(2,1)}) %reduce-scatter.5.cloned.1.call-update) | async-done | bytes 1048592 | tf_op jit(solution)/shard_map/reduce_scatter | solution.py:38
  310.7 1.6 fusion.7
  312.4 15.1 %collective-permute-done = bf16[1024,1,512]{0,2,1:T(8,128)(2,1)S(1)} collective-permute-done((bf16[1024,1,512]{0,2,1:T(8,128)(2,1)S(1)}, bf16[1024,1,512]{0,2,1:T(8,128)(2,1)S(1)}, u32[]{:S(2)}, u32[]{:S(2)}) %collective-permute-start) | collective-permute-done | bytes 1048608 | tf_op jit(solution)/shard_map/ppermute | solution.py:13
  327.6 2.6 collective-permute-start.4
  330.2 22.9 %collective-permute-done.1 = bf16[1024,1,512]{0,2,1:T(8,128)(2,1)S(1)} collective-permute-done((bf16[1024,1,512]{0,2,1:T(8,128)(2,1)S(1)}, bf16[1024,1,512]{0,2,1:T(8,128)(2,1)S(1)}, u32[]{:S(2)}, u32[]{:S(2)}) %collective-permute-start.1) | collective-permute-done | bytes 1048608 | tf_op jit(solution)/shard_map/ppermute | solution.py:13
  353.1 2.6 collective-permute-start.5
  355.7 23.6 %collective-permute-done.2 = bf16[1024,1,512]{0,2,1:T(8,128)(2,1)} collective-permute-done((bf16[1024,1,512]{0,2,1:T(8,128)(2,1)S(1)}, bf16[1024,1,512]{0,2,1:T(8,128)(2,1)}, u32[]{:S(2)}, u32[]{:S(2)}) %collective-permute-start.2) | collective-permute-done | bytes 1048608 | tf_op jit(solution)/shard_map/ppermute | solution.py:13
  379.3 2.6 collective-permute-start.6
  381.9 23.7 %collective-permute-done.3 = bf16[1024,1,512]{0,2,1:T(8,128)(2,1)} collective-permute-done((bf16[1024,1,512]{0,2,1:T(8,128)(2,1)}, bf16[1024,1,512]{0,2,1:T(8,128)(2,1)}, u32[]{:S(2)}, u32[]{:S(2)}) %collective-permute-start.3) | collective-permute-done | bytes 1048608 | tf_op jit(solution)/shard_map/ppermute | solution.py:13
  405.6 1.3 constant_dynamic-update-slice_fusion.15
  406.9 1.3 constant_dynamic-update-slice_fusion.14
  408.2 1.3 constant_dynamic-update-slice_fusion.13
  409.7 1.3 constant_dynamic-update-slice_fusion.9
  411.0 1.3 constant_dynamic-update-slice_fusion.8
  412.3 1.3 constant_dynamic-update-slice_fusion.7
  413.6 1.3 constant_dynamic-update-slice_fusion.6
  415.2 1.3 constant_dynamic-update-slice_fusion.1
  416.6 1.3 constant_dynamic-update-slice_fusion
  417.9 7.8 %fusion.8 = bf16[1024,512]{1,0:T(8,128)(2,1)} fusion(bf16[512,4096]{1,0:T(8,128)(2,1)} %all-gather.8.cloned.1.call-done, bf16[1024,1,8192]{0,2,1:T(8,128)(2,1)S(1)} %constant_dynamic-update-slice_fusion, s32[]{:T(128)S(6)} %select_n.62), kind=kOutput, calls=%fused_computation.15 | convolution fusion | flops 4295491584 | bytes 13631492 | tf_op jit(solution)/shard_map/jqk,ik->jqi/dot_general | solution.py:48
  425.9 0.4 select_reduce_fusion.1
  426.4 0.3 convert_reduce_fusion.1
  426.9 0.3 convolution_convert_fusion
  427.2 1.2 copy.28
  428.5 3.5 all-to-all-start.1
  432.1 9.6 %all-to-all-done.1 = bf16[8,4,8192]{2,1,0:T(4,128)(2,1)S(1)} async-done(((bf16[8,4,8192]{2,1,0:T(4,128)(2,1)}), bf16[8,4,8192]{2,1,0:T(4,128)(2,1)S(1)}, u32[]{:S(2)}, u32[]{:S(2)}) %all-to-all-start.1) | async-done | bytes 524320 | tf_op jit(solution)/shard_map/all_to_all | solution.py:117
  441.7 0.4 fusion.2
  442.1 0.8 reshape.265
  442.9 0.3 all-gather.16.cloned.1.call-start
  443.2 62.1 %all-gather.14.cloned.1.call-done = bf16[4096,512]{1,0:T(8,128)(2,1)} async-done(((bf16[1024,512]{1,0:T(8,128)(2,1)}), bf16[4096,512]{1,0:T(8,128)(2,1)}) %all-gather.14.cloned.1.call-update) | async-done | bytes 4194320 | tf_op jit(solution)/shard_map/all_gather | solution.py:58
  505.3 10.3 %fusion.11 = bf16[1024,512]{0,1:T(8,128)(2,1)} fusion(bf16[4096,512]{1,0:T(8,128)(2,1)} %all-gather.14.cloned.1.call-done, bf16[1024,4096]{1,0:T(8,128)(2,1)} %all-gather.10.cloned.1.call-done), kind=kOutput, calls=%fused_computation.17 | convolution fusion | flops 4295491584 | bytes 13631488 | tf_op jit(solution)/shard_map/jk,kqi->jqi/dot_general | solution.py:55
  515.8 0.3 convolution_convert_fusion.1
  516.0 1.3 copy.24
  517.3 3.7 all-to-all-start
  521.0 9.7 %all-to-all-done = bf16[8,4,8192]{2,1,0:T(4,128)(2,1)S(1)} async-done(((bf16[8,4,8192]{2,1,0:T(4,128)(2,1)}), bf16[8,4,8192]{2,1,0:T(4,128)(2,1)S(1)}, u32[]{:S(2)}, u32[]{:S(2)}) %all-to-all-start) | async-done | bytes 524320 | tf_op jit(solution)/shard_map/all_to_all | solution.py:116
  530.8 0.4 fusion.1
  531.5 1.8 all-gather.12.cloned.1.call-done
  533.3 55.8 %all-gather.16.cloned.1.call-done = bf16[1024,4096]{0,1:T(8,128)(2,1)} async-done(((bf16[1024,512]{0,1:T(8,128)(2,1)}), bf16[1024,4096]{0,1:T(8,128)(2,1)}) %all-gather.16.cloned.1.call-update) | async-done | bytes 8388624 | tf_op jit(solution)/shard_map/all_gather | solution.py:126
  589.1 6.0 fusion.13
  595.1 11.8 %psum.7 = f32[1,16,8]{2,1,0:T(8,128)S(1)} all-reduce(f32[1,16,8]{2,1,0:T(8,128)S(1)} %reshape.266), channel_id=1, replica_groups=mesh['tensor'=4,'example'=8] {'tensor'}, use_global_device_ids=true, to_apply=%region_7.8 | all-reduce | flops 128 | bytes 1024 | tf_op jit(solution)/shard_map/psum | solution.py:130
  607.1 0.7 copy.31
  (59 shorter events, 1.9 us)
Async XLA Ops:
  6.5 85.9 %copy-start = (bf16[1,512,1024]{2,1,0:T(8,128)(2,1)S(1)}, bf16[1,512,1024]{2,1,0:T(8,128)(2,1)}, u32[]{:S(2)}) copy-start(bf16[1,512,1024]{2,1,0:T(8,128)(2,1)} %param.9) | copy-start | bytes 3145732
  6.5 85.9 %all-gather.8.cloned.1.call-start = ((), (), s32[]{:S(2)}) async-start(), calls=%async_computation.4 | async-start | bytes 5242880 | tf_op jit(solution)/shard_map/all_gather | solution.py:25
  7.3 141.6 %all-gather.10.cloned.1.call-start = ((), (), s32[]{:S(2)}) async-start(), calls=%async_computation.6 | async-start | bytes 9437184 | tf_op jit(solution)/shard_map/all_gather | solution.py:26
  8.0 215.6 %reduce-scatter.3.cloned.1.call-start = ((), (), s32[]{:S(2)}) async-start(), calls=%async_computation.5 | async-start | bytes 9437184 | tf_op jit(solution)/shard_map/reduce_scatter | solution.py:29
  101.4 209.3 %reduce-scatter.5.cloned.1.call-start = ((), (), s32[]{:S(2)}) async-start(), calls=%async_computation.7 | async-start | bytes 5242880 | tf_op jit(solution)/shard_map/reduce_scatter | solution.py:38
  233.8 271.5 %all-gather.14.cloned.1.call-start = ((), (), s32[]{:S(2)}) async-start(), calls=%async_computation.9 | async-start | bytes 5242880 | tf_op jit(solution)/shard_map/all_gather | solution.py:58
  312.4 15.2 %collective-permute-start = (bf16[1024,1,512]{0,2,1:T(8,128)(2,1)S(1)}, bf16[1024,1,512]{0,2,1:T(8,128)(2,1)S(1)}, u32[]{:S(2)}, u32[]{:S(2)}) collective-permute-start(bf16[1024,1,512]{0,2,1:T(8,128)(2,1)S(1)} %fusion.7), channel_id=1, source_target_pairs={{0,1},{1,2},{2,3},{3,4},{4,5},{5,6},{6,7},{7,0},{8,9},{9,10},{10,1... | collective-permute-start | bytes 3145736 | tf_op jit(solution)/shard_map/ppermute | solution.py:13
  327.6 25.5 %collective-permute-start.1 = (bf16[1024,1,512]{0,2,1:T(8,128)(2,1)S(1)}, bf16[1024,1,512]{0,2,1:T(8,128)(2,1)S(1)}, u32[]{:S(2)}, u32[]{:S(2)}) collective-permute-start(bf16[1024,1,512]{0,2,1:T(8,128)(2,1)S(1)} %collective-permute-done), channel_id=1, source_target_pairs={{0,1},{1,2},{2,3},{3,4},{4,5},{5,6},{6,7},{7,0},{8,9},{9,10},{10,1... | collective-permute-start | bytes 3145736 | tf_op jit(solution)/shard_map/ppermute | solution.py:13
  327.6 25.5 %collective-permute-start.4 = (bf16[1024,1,512]{0,2,1:T(8,128)(2,1)S(1)}, bf16[1024,1,512]{0,2,1:T(8,128)(2,1)S(1)}, u32[]{:S(2)}, u32[]{:S(2)}) collective-permute-start(bf16[1024,1,512]{0,2,1:T(8,128)(2,1)S(1)} %fusion.7), channel_id=1, source_target_pairs={{0,7},{1,0},{2,1},{3,2},{4,3},{5,4},{6,5},{7,6},{8,15},{9,8},{10,9... | collective-permute-start | bytes 3145736 | tf_op jit(solution)/shard_map/ppermute | solution.py:15
  353.1 26.2 %copy-start.2 = (bf16[1024,1,512]{0,2,1:T(8,128)(2,1)}, bf16[1024,1,512]{0,2,1:T(8,128)(2,1)S(1)}, u32[]{:S(2)}) copy-start(bf16[1024,1,512]{0,2,1:T(8,128)(2,1)S(1)} %collective-permute-done.1) | copy-start | bytes 3145732
  353.1 26.2 %collective-permute-start.2 = (bf16[1024,1,512]{0,2,1:T(8,128)(2,1)S(1)}, bf16[1024,1,512]{0,2,1:T(8,128)(2,1)}, u32[]{:S(2)}, u32[]{:S(2)}) collective-permute-start(bf16[1024,1,512]{0,2,1:T(8,128)(2,1)S(1)} %collective-permute-done.1), channel_id=1, source_target_pairs={{0,1},{1,2},{2,3},{3,4},{4,5},{5,6},{6,7},{7,0},{8,9},{9,10},{10,1... | collective-permute-start | bytes 3145736 | tf_op jit(solution)/shard_map/ppermute | solution.py:13
  353.1 26.2 %collective-permute-start.5 = (bf16[1024,1,512]{0,2,1:T(8,128)(2,1)S(1)}, bf16[1024,1,512]{0,2,1:T(8,128)(2,1)}, u32[]{:S(2)}, u32[]{:S(2)}) collective-permute-start(bf16[1024,1,512]{0,2,1:T(8,128)(2,1)S(1)} %collective-permute-done.4), channel_id=1, source_target_pairs={{0,7},{1,0},{2,1},{3,2},{4,3},{5,4},{6,5},{7,6},{8,15},{9,8},{10,9... | collective-permute-start | bytes 3145736 | tf_op jit(solution)/shard_map/ppermute | solution.py:15
  379.3 26.3 %collective-permute-start.3 = (bf16[1024,1,512]{0,2,1:T(8,128)(2,1)}, bf16[1024,1,512]{0,2,1:T(8,128)(2,1)}, u32[]{:S(2)}, u32[]{:S(2)}) collective-permute-start(bf16[1024,1,512]{0,2,1:T(8,128)(2,1)} %collective-permute-done.2), channel_id=1, source_target_pairs={{0,1},{1,2},{2,3},{3,4},{4,5},{5,6},{6,7},{7,0},{8,9},{9,10},{10,1... | collective-permute-start | bytes 3145736 | tf_op jit(solution)/shard_map/ppermute | solution.py:13
  379.3 31.7 %collective-permute-start.6 = (bf16[1024,1,512]{0,2,1:T(8,128)(2,1)}, bf16[1024,1,512]{0,2,1:T(8,128)(2,1)}, u32[]{:S(2)}, u32[]{:S(2)}) collective-permute-start(bf16[1024,1,512]{0,2,1:T(8,128)(2,1)} %collective-permute-done.5), channel_id=1, source_target_pairs={{0,7},{1,0},{2,1},{3,2},{4,3},{5,4},{6,5},{7,6},{8,15},{9,8},{10,9... | collective-permute-start | bytes 3145736 | tf_op jit(solution)/shard_map/ppermute | solution.py:15
  381.9 33.0 %copy-start.3 = (bf16[1024,1,512]{0,2,1:T(8,128)(2,1)S(1)}, bf16[1024,1,512]{0,2,1:T(8,128)(2,1)}, u32[]{:S(2)}) copy-start(bf16[1024,1,512]{0,2,1:T(8,128)(2,1)} %copy-done.2) | copy-start | bytes 3145732
  416.5 9.2 %copy-start.4 = (bf16[16,8,1024]{2,1,0:T(8,128)(2,1)S(1)}, bf16[16,8,1024]{2,1,0:T(8,128)(2,1)}, u32[]{:S(2)}) copy-start(bf16[16,8,1024]{2,1,0:T(8,128)(2,1)} %param.14) | copy-start | bytes 786436
  416.6 9.3 %copy-start.6 = (s32[8,16]{1,0:T(8,128)S(1)}, s32[8,16]{1,0:T(8,128)}, u32[]{:S(2)}) copy-start(s32[8,16]{1,0:T(8,128)} %param.16) | copy-start | bytes 1540
  416.6 9.3 %copy-start.7 = (s32[128]{0:T(128)S(1)}, s32[128]{0:T(128)}, u32[]{:S(2)}) copy-start(s32[128]{0:T(128)} %param.17) | copy-start | bytes 1540
  416.6 9.3 %copy-start.8 = (s32[128]{0:T(128)S(1)}, s32[128]{0:T(128)}, u32[]{:S(2)}) copy-start(s32[128]{0:T(128)} %param.15) | copy-start | bytes 1540
  428.5 13.2 %all-to-all-start.1 = ((bf16[8,4,8192]{2,1,0:T(4,128)(2,1)}), bf16[8,4,8192]{2,1,0:T(4,128)(2,1)S(1)}, u32[]{:S(2)}, u32[]{:S(2)}) async-start(bf16[8,4,8192]{2,1,0:T(4,128)(2,1)} %copy.28), calls=%async_computation.3 | async-start | bytes 1048576 | tf_op jit(solution)/shard_map/all_to_all | solution.py:117
  432.0 83.7 %copy-start.5 = (bf16[16,8,1024]{2,1,0:T(8,128)(2,1)S(1)}, bf16[16,8,1024]{2,1,0:T(8,128)(2,1)}, u32[]{:S(2)}) copy-start(bf16[16,8,1024]{2,1,0:T(8,128)(2,1)} %param.13) | copy-start | bytes 786436
  432.0 101.3 %all-gather.12.cloned.1.call-start = ((), (), s32[]{:S(2)}) async-start(), calls=%async_computation.8 | async-start | bytes 1310720 | tf_op jit(solution)/shard_map/all_gather | solution.py:121
  442.9 146.1 %all-gather.16.cloned.1.call-start = ((), (), s32[]{:S(2)}) async-start(), calls=%async_computation.10 | async-start | bytes 9437184 | tf_op jit(solution)/shard_map/all_gather | solution.py:126
  505.3 102.4 %copy-start.1 = (bf16[1,512,1024]{2,1,0:T(8,128)(2,1)S(1)}, bf16[1,512,1024]{2,1,0:T(8,128)(2,1)}, u32[]{:S(2)}) copy-start(bf16[1,512,1024]{2,1,0:T(8,128)(2,1)} %param.9) | copy-start | bytes 3145732
  517.3 13.4 %all-to-all-start = ((bf16[8,4,8192]{2,1,0:T(4,128)(2,1)}), bf16[8,4,8192]{2,1,0:T(4,128)(2,1)S(1)}, u32[]{:S(2)}, u32[]{:S(2)}) async-start(bf16[8,4,8192]{2,1,0:T(4,128)(2,1)} %copy.24), calls=%async_computation | async-start | bytes 1048576 | tf_op jit(solution)/shard_map/all_to_all | solution.py:116
Sparse Core Ops, SparseCore 0:
  8.9 83.4 all-gather.7
  94.3 54.4 all-gather.9
  152.3 71.2 reduce-scatter.2
  233.9 76.7 reduce-scatter.4
  425.9 79.4 all-gather.13
  506.8 26.4 all-gather.11
  535.1 53.8 all-gather.15
